TPU v7x, 32 devices: a whole 2x2x4 slice. The times are simulated.
32 devices in a mesh: dp: 4 (over z), row: 4 (over x, core), col: 2 (over y).
Axes of the slice: x: 2, y: 2, z: 4, core: 2. Of those that a mesh axis runs over, the one named last changes fastest.
Arguments:
- tokens: bfloat16 [11664, 1152], P(('dp', 'col'), 'row'), may hold values from -6 to 6
- ln_gain: bfloat16 [2, 1152], P(None, 'row'), may hold values from 0.5 to 1.5
- ln_bias: bfloat16 [2, 1152], P(None, 'row'), may hold values from -3 to 3
- w_qkv: bfloat16 [1152, 3, 1152], P('row', None, 'col'), may hold values from -0.1875 to 0.1875
- b_qv: bfloat16 [2, 1152], P(None, 'col'), may hold values from -3 to 3
- w_out: bfloat16 [1152, 1152], P('col', 'row'), may hold values from -3 to 3
- b_out: bfloat16 [1152], P('row'), may hold values from -3 to 3
- w_up: bfloat16 [1152, 4304], P('row', 'col'), may hold values from -0.1875 to 0.1875
- b_up: bfloat16 [4304], P('col'), may hold values from -3 to 3
- w_down: bfloat16 [4304, 1152], P('col', 'row'), may hold values from -0.09375 to 0.09375
- b_down: bfloat16 [1152], P('row'), may hold values from -3 to 3
- cotangent: bfloat16 [11664, 1152], P(('dp', 'col'), 'row'), may hold values from -6 to 6
Outputs:
- output: bfloat16 [11664, 1152], P(('dp', 'col'), 'row')
- input_grad: bfloat16 [11664, 1152], P(('dp', 'col'), 'row')
- d_ln_gain: float32 [2, 1152], P(None, 'row')
- d_ln_bias: float32 [2, 1152], P(None, 'row')
- d_w_qkv: float32 [1152, 3, 1152], P(('row', 'dp'), None, 'col')
- d_b_qv: float32 [2, 1152], P(None, 'col')
- d_w_out: float32 [1152, 1152], P(('col', 'dp'), 'row')
- d_b_out: float32 [1152], P('row')
- d_w_up: float32 [1152, 4304], P(('row', 'dp'), 'col')
- d_b_up: float32 [4304], P('col')
- d_w_down: float32 [4304, 1152], P('col', ('row', 'dp'))
- d_b_down: float32 [1152], P('row')
All inputs are finite; a program needn't handle non-finite values.
Results may differ from a plain program's by a relative error of at most 0.018.
Values may be sent and summed in bfloat16 or wider, within the bound.
A program may use at most 192 MiB of HBM per device.

v0:
```python
import jax
import jax.numpy as jnp
from jax import lax
from jax.sharding import PartitionSpec as P

HD = 72
SEQ = 729
epsilon = 1e-06


def gelu_tanh(values):
    return (
        0.5
        * values
        * (1.0 + jnp.tanh(0.7978845608028654 * (values + 0.044715 * values * values * values)))
    )


def row_sums(first_part, second_part):
    return lax.psum((first_part, second_part), "row")


def norm_forward(values, gain, shift):
    full_width = values.shape[1] * lax.axis_size("row")
    row_total, square_total = row_sums(jnp.sum(values, axis=1), jnp.sum(values * values, axis=1))
    row_mean = row_total / full_width
    norm_scale = lax.rsqrt(square_total / full_width - row_mean * row_mean + epsilon)
    normed = (values - row_mean[:, None]) * norm_scale[:, None]
    return (normed, norm_scale, normed * gain + shift)


def norm_backward(incoming, normed, norm_scale, gain):
    full_width = normed.shape[1] * lax.axis_size("row")
    scaled = incoming * gain
    scaled_total, cross_total = row_sums(jnp.sum(scaled, axis=1), jnp.sum(scaled * normed, axis=1))
    back_grad = norm_scale[:, None] * (
        scaled - scaled_total[:, None] / full_width - normed * (cross_total[:, None] / full_width)
    )
    return (back_grad, jnp.sum(incoming * normed, axis=0), jnp.sum(incoming, axis=0))


def gather_tokens(pieces):
    return lax.all_gather(pieces, "col", axis=0, tiled=True)


def sum_over_col(row_term, total_rows):
    return lax.psum_scatter(
        row_term(jnp.int32(0), lax.axis_size("col") * (total_rows // lax.axis_size("col"))),
        "col",
        scatter_dimension=0,
        tiled=True,
    )


def project_in(normed_low, weight):
    rows_all = gather_tokens(normed_low)

    def row_term(first_row, row_count):
        return jnp.dot(rows_all, weight, preferred_element_type=jnp.float32)

    result = lax.psum_scatter(
        row_term(jnp.int32(0), lax.axis_size("row") * (rows_all.shape[0] // lax.axis_size("row"))),
        "row",
        scatter_dimension=0,
        tiled=True,
    )
    return (result, rows_all)


def project_in_back(grad_low, saved_in, weight):
    grads_all = lax.all_gather(grad_low, "row", axis=0, tiled=True)
    weight_grad = lax.dot_general(
        saved_in, grads_all, (((0,), (0,)), ((), ())), preferred_element_type=jnp.float32
    )

    def row_term(first_row, row_count):
        return lax.dot_general(
            grads_all, weight, (((1,), (1,)), ((), ())), preferred_element_type=jnp.float32
        )

    input_grad = sum_over_col(row_term, grads_all.shape[0])
    return (input_grad, weight_grad)


def project_out(inner_low, weight):
    inner_all = lax.all_gather(inner_low, "row", axis=0, tiled=True)

    def row_term(first_row, row_count):
        return jnp.dot(inner_all, weight, preferred_element_type=jnp.float32)

    result = lax.psum_scatter(
        row_term(
            jnp.int32(0), inner_all.shape[0] // lax.axis_size("col") * lax.axis_size("col")
        ).astype(jnp.bfloat16),
        "col",
        scatter_dimension=0,
        tiled=True,
    ).astype(jnp.float32)
    return (result, inner_all)


def project_out_back(grad_low, inner_all, weight):
    grads_all = gather_tokens(grad_low)
    weight_grad = lax.dot_general(
        inner_all, grads_all, (((0,), (0,)), ((), ())), preferred_element_type=jnp.float32
    )
    bias_grad = jnp.sum(grad_low, axis=0, dtype=jnp.float32)

    def row_term(first_row, row_count):
        return lax.dot_general(
            grads_all, weight, (((1,), (1,)), ((), ())), preferred_element_type=jnp.float32
        )

    inner_grad = lax.psum_scatter(
        row_term(jnp.int32(0), lax.axis_size("row") * (grads_all.shape[0] // lax.axis_size("row"))),
        "row",
        scatter_dimension=0,
        tiled=True,
    )
    return (inner_grad, weight_grad, bias_grad)


def attend_forward(image_block):
    queries = image_block[:, 0]
    keys_in = image_block[:, 1]
    values = image_block[:, 2]
    scores = jnp.einsum(
        "qhd,khd->hqk", queries, keys_in, preferred_element_type=jnp.float32
    ) * HD ** (-0.5)
    row_top = jnp.max(scores, axis=-1, keepdims=True)
    exponent = jnp.exp(scores - row_top)
    row_total = jnp.sum(exponent, axis=-1, keepdims=True)
    weights = (exponent / row_total).astype(jnp.bfloat16)
    heads_out = jnp.einsum("hqk,khd->qhd", weights, values, preferred_element_type=jnp.float32)
    return (heads_out.astype(jnp.bfloat16), (row_top + jnp.log(row_total))[..., 0])


def attend_backward(image_block, logsum, grad_heads):
    queries = image_block[:, 0]
    keys_in = image_block[:, 1]
    values = image_block[:, 2]
    scores = jnp.einsum(
        "qhd,khd->hqk", queries, keys_in, preferred_element_type=jnp.float32
    ) * HD ** (-0.5)
    soft_probs = jnp.exp(scores - logsum[..., None])
    weights = soft_probs.astype(jnp.bfloat16)
    value_grad = jnp.einsum("hqk,qhd->khd", weights, grad_heads, preferred_element_type=jnp.float32)
    prob_grad = jnp.einsum("qhd,khd->hqk", grad_heads, values, preferred_element_type=jnp.float32)
    row_delta = jnp.sum(soft_probs * prob_grad, axis=-1, keepdims=True)
    score_grad = (soft_probs * (prob_grad - row_delta)).astype(jnp.bfloat16)
    query_grad = jnp.einsum(
        "hqk,khd->qhd", score_grad, keys_in, preferred_element_type=jnp.float32
    ) * HD ** (-0.5)
    key_grad = jnp.einsum(
        "hqk,qhd->khd", score_grad, queries, preferred_element_type=jnp.float32
    ) * HD ** (-0.5)
    return jnp.stack([query_grad, key_grad, value_grad], axis=1).astype(jnp.bfloat16)


def place_block(block, position, part_count):
    block_size = block.shape[-1]
    zero_vector = jnp.zeros(block.shape[:-1] + (block_size * part_count,), jnp.float32)
    return lax.dynamic_update_slice_in_dim(
        zero_vector, block, position * block_size, block.ndim - 1
    )


def take_block(whole_vector, position, block_size):
    return lax.dynamic_slice_in_dim(
        whole_vector, position * block_size, block_size, whole_vector.ndim - 1
    )


def shards(
    tokens, ln_gain, ln_bias, w_qkv, b_qv, w_out, b_out, w_up, b_up, w_down, b_down, cotangent
):
    inputs = tokens.astype(jnp.float32)
    gain_rows = ln_gain.astype(jnp.float32)
    shift_rows = ln_bias.astype(jnp.float32)
    row_width = tokens.shape[1]
    head_width = b_qv.shape[1]
    heads_here = head_width // HD
    qkv_weight = w_qkv.reshape(row_width, 3 * head_width)
    normed_one, scale_one, first_out = norm_forward(inputs, gain_rows[0], shift_rows[0])
    projected, saved_one = project_in(first_out.astype(jnp.bfloat16), qkv_weight)
    qv_bias = b_qv.astype(jnp.float32)
    bias_rows = jnp.stack([qv_bias[0], jnp.zeros_like(qv_bias[0]), qv_bias[1]])
    images = projected.shape[0] // SEQ
    triple = (projected.reshape(-1, 3, head_width) + bias_rows).astype(jnp.bfloat16)
    triple = triple.reshape(images, SEQ, 3, heads_here, HD)
    heads_low, logsum = lax.map(attend_forward, triple)
    heads_low = heads_low.reshape(-1, head_width)
    attn_part, heads_all = project_out(heads_low, w_out)
    residual = inputs + attn_part + b_out.astype(jnp.float32)
    normed_two, scale_two, second_out = norm_forward(residual, gain_rows[1], shift_rows[1])
    up_total, saved_two = project_in(second_out.astype(jnp.bfloat16), w_up)
    up_value = up_total + b_up.astype(jnp.float32)
    hidden_act, gelu_pull = jax.vjp(gelu_tanh, up_value)
    down_part, hidden_all = project_out(hidden_act.astype(jnp.bfloat16), w_down)
    output = (residual + down_part + b_down.astype(jnp.float32)).astype(jnp.bfloat16)
    act_grad, down_grad, down_bias_grad = project_out_back(cotangent, hidden_all, w_down)
    up_grad = gelu_pull(act_grad)[0].astype(jnp.bfloat16)
    up_bias_grad = jnp.sum(up_grad, axis=0, dtype=jnp.float32)
    second_grad, up_weight_grad = project_in_back(up_grad, saved_two, w_up)
    back_two, gain_two, shift_two = norm_backward(second_grad, normed_two, scale_two, gain_rows[1])
    residual_grad = cotangent.astype(jnp.float32) + back_two
    heads_grad, out_grad, out_bias_grad = project_out_back(
        residual_grad.astype(jnp.bfloat16), heads_all, w_out
    )
    heads_grad = heads_grad.astype(jnp.bfloat16).reshape(images, SEQ, heads_here, HD)
    triple_grad = lax.map(
        lambda image_set: attend_backward(image_set[0], image_set[1], image_set[2]),
        (triple, logsum, heads_grad),
    )
    triple_grad = triple_grad.reshape(-1, 3 * head_width)
    triple_bias_grad = jnp.sum(triple_grad.reshape(-1, 3, head_width), axis=0, dtype=jnp.float32)
    first_grad, triple_weight_grad = project_in_back(triple_grad, saved_one, qkv_weight)
    back_one, gain_one, shift_one = norm_backward(first_grad, normed_one, scale_one, gain_rows[0])
    input_grad = (residual_grad + back_one).astype(jnp.bfloat16)
    row_here = lax.axis_index("row")
    col_here = lax.axis_index("col")
    row_block = jnp.stack([gain_one, gain_two, shift_one, shift_two, out_bias_grad, down_bias_grad])
    row_full = place_block(row_block, row_here, lax.axis_size("row"))
    qv_full = place_block(triple_bias_grad[::2], col_here, lax.axis_size("col"))
    up_full = place_block(up_bias_grad, col_here, lax.axis_size("col"))
    row_summed, qv_summed, up_summed = lax.psum((row_full, qv_full, up_full), ("dp", "row", "col"))
    row_vectors = take_block(row_summed, row_here, row_width)
    qv_vectors = take_block(qv_summed, col_here, head_width)
    up_vector = take_block(up_summed, col_here, up_bias_grad.shape[0])
    triple_shaped = triple_weight_grad.reshape(row_width, 3, head_width)
    triple_total, out_total, up_weight_total, down_total = (
        lax.psum_scatter(
            triple_shaped.astype(jnp.bfloat16), "dp", scatter_dimension=0, tiled=True
        ).astype(jnp.float32),
        lax.psum_scatter(
            out_grad.astype(jnp.bfloat16), "dp", scatter_dimension=0, tiled=True
        ).astype(jnp.float32),
        lax.psum_scatter(
            up_weight_grad.astype(jnp.bfloat16), "dp", scatter_dimension=0, tiled=True
        ).astype(jnp.float32),
        lax.psum_scatter(
            down_grad.astype(jnp.bfloat16), "dp", scatter_dimension=1, tiled=True
        ).astype(jnp.float32),
    )
    return (
        output,
        input_grad,
        row_vectors[0:2],
        row_vectors[2:4],
        triple_total,
        qv_vectors,
        out_total,
        row_vectors[4],
        up_weight_total,
        up_vector,
        down_total,
        row_vectors[5],
    )


def solution(mesh):
    placed = (
        P(("dp", "col"), "row"),
        P(None, "row"),
        P(None, "row"),
        P("row", None, "col"),
        P(None, "col"),
        P("col", "row"),
        P("row"),
        P("row", "col"),
        P("col"),
        P("col", "row"),
        P("row"),
        P(("dp", "col"), "row"),
    )
    return jax.shard_map(
        shards,
        mesh=mesh,
        in_specs=placed,
        out_specs=(
            P(("dp", "col"), "row"),
            P(("dp", "col"), "row"),
            P(None, "row"),
            P(None, "row"),
            P(("row", "dp"), None, "col"),
            P(None, "col"),
            P(("col", "dp"), "row"),
            P("row"),
            P(("row", "dp"), "col"),
            P("col"),
            P("col", ("row", "dp")),
            P("row"),
        ),
        check_vma=False,
    )
```

profile of v0, /device:TPU:0, one launch (start us, length us, event | category | flops | bytes accessed | tf_op | source)
XLA Modules:
  0.0 1888.4 jit_solution(2578188602203052811)
XLA Ops:
  10.2 12.7 all-reduce.18
  27.7 28.1 %all-gather.17.cloned.1.call-done = bf16[2,1458,288]{1,2,0:T(8,128)(2,1)} async-done(((bf16[1,1458,288]{1,2,0:T(8,128)(2,1)}), bf16[2,1458,288]{1,2,0:T(8,128)(2,1)}) %all-gather.17.cloned.1.call-update) | async-done | bytes 1679632 | tf_op jit(solution)/shard_map/all_gather | solution.py:43
  64.9 12.0 fusion.47
  76.9 181.4 %fusion = f32[736,1728]{1,0:T(8,128)} fusion(f32[2916,1728]{1,0:T(8,128)} %fusion.47), kind=kCustom, calls=%all-reduce-scatter | all-reduce-scatter fusion | flops 5087233 | bytes 25243136
  262.4 14.1 concatenate.2
  290.8 7.6 multiply_reduce_fusion.1
  298.4 9.2 fusion.3
  307.6 9.3 fusion.32
  317.7 32.9 %all-gather.19.cloned.1.call-done = bf16[4,729,576]{1,2,0:T(8,128)(2,1)} async-done(((bf16[1,729,576]{1,2,0:T(8,128)(2,1)}), bf16[4,729,576]{1,2,0:T(8,128)(2,1)}) %all-gather.19.cloned.1.call-update) | async-done | bytes 3359248 | tf_op jit(solution)/shard_map/all_gather | solution.py:86
  350.6 6.5 copy.48
  357.1 7.8 reshape.95
  371.1 10.4 all-gather.25.cloned.1.call-done
  387.4 13.8 fusion.49
  401.2 36.7 %all-reduce.26.cloned.1.call-done = bf16[2916,288]{0,1:T(8,128)(2,1)} async-done(((bf16[2916,288]{0,1:T(8,128)(2,1)}), bf16[2916,288]{0,1:T(8,128)(2,1)}) %all-reduce.26.cloned.1.call-update) | async-done | bytes 1679632
  439.9 10.7 all-reduce.17
  454.0 218.1 %fusion.2 = f32[736,2152]{1,0:T(8,128)} fusion(f32[2916,2152]{1,0:T(8,128)} %fusion.49), kind=kCustom, calls=%all-reduce-scatter.2 | all-reduce-scatter fusion | flops 6335489 | bytes 31436928
  684.4 13.3 fusion.48
  697.7 219.8 %fusion.1 = f32[736,2152]{1,0:T(8,128)} fusion(f32[2916,2152]{1,0:T(8,128)} %fusion.48), kind=kCustom, calls=%all-reduce-scatter.1 | all-reduce-scatter fusion | flops 6335489 | bytes 31436928
  919.8 17.6 concatenate.4
  937.4 17.6 concatenate.3
  955.0 11.7 convert_reduce_fusion
  968.0 82.1 %all-gather.27.cloned.1.call-done = bf16[4,729,2152]{2,1,0:T(8,128)(2,1)} async-done(((bf16[1,729,2152]{2,1,0:T(8,128)(2,1)}), bf16[4,729,2152]{2,1,0:T(8,128)(2,1)}) %all-gather.27.cloned.1.call-update) | async-done | bytes 12550480 | tf_op jit(solution)/shard_map/all_gather | solution.py:71
  1050.1 18.0 reshape.103
  1068.1 10.7 fusion.50
  1079.0 56.0 %all-gather.23.cloned.1.call-done = bf16[4,729,2152]{2,1,0:T(8,128)(2,1)} async-done(((bf16[1,729,2152]{2,1,0:T(8,128)(2,1)}), bf16[4,729,2152]{2,1,0:T(8,128)(2,1)}) %all-gather.23.cloned.1.call-update) | async-done | bytes 12550480 | tf_op jit(solution)/shard_map/all_gather | solution.py:86
  1135.0 17.4 reshape.99
  1152.5 13.6 convolution_convert_fusion.2
  1166.2 62.4 %all-reduce.30.cloned.1.call-done = f32[2916,288]{0,1:T(8,128)} async-done(((f32[2916,288]{0,1:T(8,128)}), f32[2916,288]{0,1:T(8,128)}) %all-reduce.30.cloned.1.call-update) | async-done | bytes 3359248
  1231.9 11.5 all-reduce.16
  1243.3 41.8 %all-reduce.28.cloned.1.call-done = bf16[2916,288]{0,1:T(8,128)(2,1)} async-done(((bf16[2916,288]{0,1:T(8,128)(2,1)}), bf16[2916,288]{0,1:T(8,128)(2,1)}) %all-reduce.28.cloned.1.call-update) | async-done | bytes 1679632
  1293.5 28.9 %all-gather.29.cloned.1.call-done = bf16[2,1458,288]{1,2,0:T(8,128)(2,1)} async-done(((bf16[1,1458,288]{1,2,0:T(8,128)(2,1)}), bf16[2,1458,288]{1,2,0:T(8,128)(2,1)}) %all-gather.29.cloned.1.call-update) | async-done | bytes 1679632 | tf_op jit(solution)/shard_map/all_gather | solution.py:43
  1332.3 6.2 fusion.51
  1338.5 120.7 %all-reduce.35 = bf16[2916,576]{0,1:T(8,128)(2,1)} all-reduce(f32[2916,576]{0,1:T(8,128)} %fusion.51), channel_id=8, replica_groups=mesh['dp'=4,'row'=4,'col'=2] {'row'}, use_global_device_ids=true, to_apply=%region_20.21.clone | all-reduce | flops 1679616 | bytes 10077696
  1460.8 12.3 multiply_reduce_fusion
  1473.1 12.8 multiply_convert_fusion
  1490.4 7.9 fusion.33
  1504.9 10.5 convolution_convert_fusion.1
  1515.5 11.8 convolution_convert_fusion
  1532.8 42.1 %all-gather.31.cloned.1.call-done = bf16[4,729,1728]{2,1,0:T(8,128)(2,1)} async-done(((bf16[1,729,1728]{2,1,0:T(8,128)(2,1)}), bf16[4,729,1728]{2,1,0:T(8,128)(2,1)}) %all-gather.31.cloned.1.call-update) | async-done | bytes 10077712 | tf_op jit(solution)/shard_map/all_gather | solution.py:71
  1574.9 14.8 reshape.107
  1589.7 8.9 convolution_convert_fusion.4
  1605.8 9.5 fusion.52
  1619.4 19.5 %reduce-scatter.23.cloned.1.call-done = bf16[2152,72]{0,1:T(8,128)(2,1)} async-done(((bf16[2152,288]{0,1:T(8,128)(2,1)}), bf16[2152,72]{0,1:T(8,128)(2,1)}) %reduce-scatter.23.cloned.1.call-update) | async-done | bytes 309904
  1642.8 19.0 %reduce-scatter.19.cloned.1.call-done = bf16[144,288]{1,0:T(8,128)(2,1)} async-done(((bf16[576,288]{1,0:T(8,128)(2,1)}), bf16[144,288]{1,0:T(8,128)(2,1)}) %reduce-scatter.19.cloned.1.call-update) | async-done | bytes 82960 | tf_op jit(solution)/shard_map/reduce_scatter | solution.py:235
  1663.4 64.7 %all-reduce.34.cloned.1.call-done = bf16[288,3,576]{2,1,0:T(4,128)(2,1)} async-done(((bf16[288,3,576]{2,1,0:T(4,128)(2,1)}), bf16[288,3,576]{2,1,0:T(4,128)(2,1)}) %all-reduce.34.cloned.1.call-update) | async-done | bytes 995344
  1730.0 90.7 %all-reduce.32.cloned.1.call-done = f32[2916,288]{0,1:T(8,128)} async-done(((f32[2916,288]{0,1:T(8,128)}), f32[2916,288]{0,1:T(8,128)}) %all-reduce.32.cloned.1.call-update) | async-done | bytes 3359248
  1823.7 40.5 %all-reduce.14 = (f32[6,1152]{1,0:T(8,128)S(1)}, f32[2,1152]{1,0:T(2,128)S(1)}, f32[4304]{0:T(1024)S(1)}) all-reduce(f32[6,1152]{1,0:T(8,128)S(1)} %dynamic_update_slice.18, f32[2,1152]{1,0:T(2,128)S(1)} %dynamic_update_slice.19, f32[4304]{0:T(1024)S(1)} %dynamic_update_slice.20), channel_id=1, replica_groups=mesh['dp'=4,'row'=4,'col'=2] {'dp','row','col'}, use_global_device_ids=true, to_apply=%region_33.34 | all-reduce | flops 13520 | bytes 108160 | tf_op jit(solution)/shard_map/psum | solution.py:226
  1865.6 10.9 all-reduce.15
  (167 shorter events, 134.5 us)
Async XLA Ops:
  7.2 677.2 %copy-start = (bf16[288,2152]{1,0:T(8,128)(2,1)S(1)}, bf16[288,2152]{1,0:T(8,128)(2,1)}, u32[]{:S(2)}) copy-start(bf16[288,2152]{1,0:T(8,128)(2,1)} %param.19) | copy-start | bytes 3718660
  7.2 18.9 copy-start.10
  7.2 48.7 %all-gather.17.cloned.1.call-start = ((), (), s32[]{:S(2)}) async-start(), calls=%async_computation.4 | async-start | bytes 2654208 | tf_op jit(solution)/shard_map/all_gather | solution.py:43
  8.8 18.9 %copy-start.18 = (bf16[2,576]{1,0:T(2,128)(2,1)S(1)}, bf16[2,576]{1,0:T(2,128)(2,1)}, u32[]{:S(2)}) copy-start(bf16[2,576]{1,0:T(2,128)(2,1)} %param.16) | copy-start | bytes 6916
  22.9 0.6 copy-start.12
  22.9 0.6 copy-start.14
  23.0 0.6 copy-start.16
  26.0 324.6 %all-gather.19.cloned.1.call-start = ((), (), s32[]{:S(2)}) async-start(), calls=%async_computation.5 | async-start | bytes 4423680 | tf_op jit(solution)/shard_map/all_gather | solution.py:86
  64.9 12.0 copy-start.6
  76.9 184.3 %copy-start.20 = (u32[32]{0:T(128)S(1)}, u32[32]{0:T(128)}, u32[]{:S(2)}) copy-start(u32[32]{0:T(128)} %constant.88) | copy-start | bytes 388
  259.2 3.2 collective-permute-start
  290.8 7.6 copy-start.3
  316.9 64.7 %all-gather.25.cloned.1.call-start = ((), (), s32[]{:S(2)}) async-start(), calls=%async_computation.8 | async-start | bytes 2654208 | tf_op jit(solution)/shard_map/all_gather | solution.py:43
  317.6 120.3 %all-reduce.26.cloned.1.call-start = ((), (), s32[]{:S(2)}) async-start(), calls=%async_computation.12 | async-start | bytes 3391488
  357.1 7.8 copy-start.11
  364.9 5.0 copy-start.24
  364.9 5.6 copy-start.21
  369.7 304.9 %all-gather.21.cloned.1.call-start = ((), (), s32[]{:S(2)}) async-start(), calls=%async_computation.6 | async-start | bytes 2654208 | tf_op jit(solution)/shard_map/all_gather | solution.py:43
  387.4 50.6 %copy-start.2 = (bf16[1458,288]{0,1:T(8,128)(2,1)S(1)}, bf16[1458,288]{0,1:T(8,128)(2,1)}, u32[]{:S(2)}) copy-start(bf16[1458,288]{0,1:T(8,128)(2,1)} %param.12) | copy-start | bytes 2519428
  453.9 596.1 %all-gather.27.cloned.1.call-start = ((), (), s32[]{:S(2)}) async-start(), calls=%async_computation.9 | async-start | bytes 16015360 | tf_op jit(solution)/shard_map/all_gather | solution.py:71
  673.0 246.8 %collective-permute-start.2 = (f32[21,2152]{1,0:T(8,128)S(1)}, f32[21,2152]{1,0:T(8,128)S(1)}, u32[]{:S(2)}, u32[]{:S(2)}) collective-permute-start(f32[21,2152]{1,0:T(8,128)S(1)} %slice.78), channel_id=1, source_target_pairs={{0,2},{2,4},{4,6},{1,3},{3,5},{5,7},{8,10},{10,12},{12,14},{9,11},... | collective-permute-start | bytes 542312
  697.7 222.1 %copy-start.19 = (bf16[2152]{0:T(1024)(128)(2,1)S(1)}, bf16[2152]{0:T(1024)(128)(2,1)}, u32[]{:S(2)}) copy-start(bf16[2152]{0:T(1024)(128)(2,1)} %param.20) | copy-start | bytes 12916
  918.5 19.0 %collective-permute-start.1 = (f32[21,2152]{1,0:T(8,128)S(1)}, f32[21,2152]{1,0:T(8,128)S(1)}, u32[]{:S(2)}, u32[]{:S(2)}) collective-permute-start(f32[21,2152]{1,0:T(8,128)S(1)} %slice.77), channel_id=1, source_target_pairs={{0,2},{2,4},{4,6},{1,3},{3,5},{5,7},{8,10},{10,12},{12,14},{9,11},... | collective-permute-start | bytes 542312
  966.8 168.3 %all-gather.23.cloned.1.call-start = ((), (), s32[]{:S(2)}) async-start(), calls=%async_computation.7 | async-start | bytes 16015360 | tf_op jit(solution)/shard_map/all_gather | solution.py:86
  967.5 261.1 %all-reduce.30.cloned.1.call-start = ((), (), s32[]{:S(2)}) async-start(), calls=%async_computation.14 | async-start | bytes 6782976
  1078.8 73.7 %copy-start.9 = (bf16[2152,288]{0,1:T(8,128)(2,1)S(1)}, bf16[2152,288]{0,1:T(8,128)(2,1)}, u32[]{:S(2)}) copy-start(bf16[2152,288]{0,1:T(8,128)(2,1)} %param.21) | copy-start | bytes 3718660
  1078.8 206.3 %all-reduce.28.cloned.1.call-start = ((), (), s32[]{:S(2)}) async-start(), calls=%async_computation.13 | async-start | bytes 3391488
  1152.5 13.7 copy-start.22
  1166.1 119.0 %copy-start.8 = (bf16[1458,288]{0,1:T(8,128)(2,1)S(1)}, bf16[1458,288]{0,1:T(8,128)(2,1)}, u32[]{:S(2)}) copy-start(bf16[1458,288]{0,1:T(8,128)(2,1)} %param.23) | copy-start | bytes 2519428
  1166.1 156.3 %all-gather.29.cloned.1.call-start = ((), (), s32[]{:S(2)}) async-start(), calls=%async_computation.10 | async-start | bytes 2654208 | tf_op jit(solution)/shard_map/all_gather | solution.py:43
  1290.5 1.3 copy-start.5
  1292.8 282.1 %all-gather.31.cloned.1.call-start = ((), (), s32[]{:S(2)}) async-start(), calls=%async_computation.11 | async-start | bytes 13189120 | tf_op jit(solution)/shard_map/all_gather | solution.py:71
  1473.1 12.8 copy-start.4
  1498.3 1.9 copy-start.7
  1504.7 112.9 %reduce-scatter.21.cloned.1.call-start = ((), (), s32[]{:S(2)}) async-start(), calls=%async_computation.17 | async-start | bytes 1566720
  1515.4 123.5 %reduce-scatter.23.cloned.1.call-start = ((), (), s32[]{:S(2)}) async-start(), calls=%async_computation.18 | async-start | bytes 1566720
  1527.3 134.5 %reduce-scatter.19.cloned.1.call-start = ((), (), s32[]{:S(2)}) async-start(), calls=%async_computation.3 | async-start | bytes 552960 | tf_op jit(solution)/shard_map/reduce_scatter | solution.py:235
  1532.6 195.5 %all-reduce.34.cloned.1.call-start = ((), (), s32[]{:S(2)}) async-start(), calls=%async_computation.16 | async-start | bytes 2949120
  1605.5 215.2 %all-reduce.32.cloned.1.call-start = ((), (), s32[]{:S(2)}) async-start(), calls=%async_computation.15 | async-start | bytes 6782976
  1615.3 0.7 copy-start.23
  1640.8 180.0 %copy-start.13 = (f32[1458]{0:T(1024)S(1)}, f32[1458]{0:T(1024)}, u32[]{:S(2)}) copy-start(f32[1458]{0:T(1024)} %copy-done.12) | copy-start | bytes 17500
  1640.8 180.0 %copy-start.15 = (f32[1458]{0:T(1024)S(1)}, f32[1458]{0:T(1024)}, u32[]{:S(2)}) copy-start(f32[1458]{0:T(1024)} %copy-done.14) | copy-start | bytes 17500
  1640.8 179.9 %copy-start.17 = (f32[288]{0:T(512)S(1)}, f32[288]{0:T(512)}, u32[]{:S(2)}) copy-start(f32[288]{0:T(512)} %copy-done.16) | copy-start | bytes 3460
  1877.2 4.4 copy-start.1
Sparse Core Ops, SparseCore 0:
  26.1 29.7 all-gather.16
  317.0 33.4 all-gather.18
  352.1 29.3 all-gather.24
  383.7 54.1 all-reduce.25
  454.1 29.0 all-gather.20
  966.9 83.1 all-gather.26
  1051.6 83.3 all-gather.22
  1137.4 91.1 all-reduce.29
  1230.9 54.1 all-reduce.27
  1292.9 29.4 all-gather.28
  1504.8 70.0 all-gather.30
  1577.1 30.2 reduce-scatter.20
  1609.7 29.1 reduce-scatter.22
  1641.6 20.1 reduce-scatter.18
  1664.0 64.0 all-reduce.33
  1730.3 90.4 all-reduce.31
where the time goes:
time: 1900 us; the launch traced here: 1890 us
  blocking collectives  826 us (43%)
  waiting for transfers between devices  617 us (32%)
  local copies, waits for them, and re-layouts  186 us (10%)
  matrix products  162 us (9%)
  other arithmetic  73.3 us (4%)
    unnamed x4, blocking collectives  740 us
    unnamed x26, waiting for transfers between devices  317 us
    unnamed x71, local copies, waits for them, and re-layouts  144 us
    all_gather x2, waiting for transfers between devices, project_in_back(): grads_all = lax.all_gather(grad_low, 'row', axis=0, tiled=True)  124 us
    all_gather x2, waiting for transfers between devices, project_out(): inner_all = lax.all_gather(inner_low, 'row', axis=0, tiled=True)  88.9 us
    all_gather x4, waiting for transfers between devices, gather_tokens(): return lax.all_gather(pieces, 'col', axis=0, tiled=True)  67.5 us
    psum x4, blocking collectives, row_sums(): return lax.psum((first_part, second_part), 'row')  45.8 us
    psum x1, blocking collectives, shards(): lax.psum((row_full, qv_full, up_full), ('dp', 'row', 'col'))  40.5 us
  transfers between devices with their start and end apart: 19, of which 14 were waited for; matrix products, arithmetic and copies ran while one was open for 35% of the time, Pallas kernels for 0%

commit v1 on v0

--- a/solution.py
+++ b/solution.py
@@ -83,7 +83,15 @@
 
 
 def project_out(inner_low, weight):
-    inner_all = lax.all_gather(inner_low, "row", axis=0, tiled=True)
+    ways, here = (lax.axis_size("row"), lax.axis_index("row"))
+    grown, reach = (inner_low, 1)
+    while reach < ways:
+        theirs = lax.ppermute(grown, "row", [(d, d ^ reach) for d in range(ways)])
+        mine_first = jnp.concatenate([grown, theirs], axis=0)
+        theirs_first = jnp.concatenate([theirs, grown], axis=0)
+        grown = jnp.where(here & reach == 0, mine_first, theirs_first)
+        reach = 2 * reach
+    inner_all = grown
 
     def row_term(first_row, row_count):
         return jnp.dot(inner_all, weight, preferred_element_type=jnp.float32)

time: 1900 us -> 1890 us (level)
  local copies, waits for them, and re-layouts: 186 us -> 154 us
    ppermute x0 -> x4, waiting for transfers between devices: none -> 91.6 us  [project_out(): theirs = lax.ppermute(grown, 'row', [(d, d ^ reach) for d in range(ways)])]
    all_gather x2 -> x0, waiting for transfers between devices: 88.9 us -> none  [project_out(): inner_all = lax.all_gather(inner_low, 'row', axis=0, tiled=True)]
    all_gather x2, waiting for transfers between devices: 124 us -> 164 us  [project_in_back(): grads_all = lax.all_gather(grad_low, 'row', axis=0, tiled=True)]
    unnamed x26 -> x24, waiting for transfers between devices: 317 us -> 281 us
    unnamed x71 -> x75, local copies, waits for them, and re-layouts: 144 us -> 119 us
  transfers between devices with their start and end apart: 19 -> 21, of which waited for: 14 -> 15; matrix products, arithmetic and copies ran while one was open for 35% -> 35% of each run, Pallas kernels for 0% -> 0%
where the time goes in v1:
time: 1890 us; the launch traced here: 1880 us
  blocking collectives  826 us (44%)
  waiting for transfers between devices  613 us (32%)
  matrix products  171 us (9%)
  local copies, waits for them, and re-layouts  154 us (8%)
  other arithmetic  86.1 us (5%)
    unnamed x4, blocking collectives  740 us
    unnamed x24, waiting for transfers between devices  281 us
    all_gather x2, waiting for transfers between devices, project_in_back(): grads_all = lax.all_gather(grad_low, 'row', axis=0, tiled=True)  164 us
    unnamed x75, local copies, waits for them, and re-layouts  119 us
    ppermute x4, waiting for transfers between devices, project_out(): theirs = lax.ppermute(grown, 'row', [(d, d ^ reach) for d in range(ways)])  91.6 us
    all_gather x4, waiting for transfers between devices, gather_tokens(): return lax.all_gather(pieces, 'col', axis=0, tiled=True)  57.1 us
    psum x4, blocking collectives, row_sums(): return lax.psum((first_part, second_part), 'row')  45.5 us
    psum x1, blocking collectives, shards(): lax.psum((row_full, qv_full, up_full), ('dp', 'row', 'col'))  40.5 us
  transfers between devices with their start and end apart: 21, of which 15 were waited for; matrix products, arithmetic and copies ran while one was open for 35% of the time, Pallas kernels for 0%

profile of v1, /device:TPU:0, one launch (start us, length us, event | category | flops | bytes accessed | tf_op | source)
XLA Modules:
  0.0 1881.0 jit_solution(10700760694007215343)
XLA Ops:
  10.2 12.7 all-reduce.18
  27.7 28.1 %all-gather.13.cloned.1.call-done = bf16[2,1458,288]{1,2,0:T(8,128)(2,1)} async-done(((bf16[1,1458,288]{1,2,0:T(8,128)(2,1)}), bf16[2,1458,288]{1,2,0:T(8,128)(2,1)}) %all-gather.13.cloned.1.call-update) | async-done | bytes 1679632 | tf_op jit(solution)/shard_map/all_gather | solution.py:43
  64.9 12.0 fusion.50
  76.9 181.5 %fusion = f32[736,1728]{1,0:T(8,128)} fusion(f32[2916,1728]{1,0:T(8,128)} %fusion.50), kind=kCustom, calls=%all-reduce-scatter | all-reduce-scatter fusion | flops 5087233 | bytes 25243136
  262.5 14.1 concatenate.34
  281.9 6.1 copy.45
  290.9 7.5 multiply_reduce_fusion.1
  298.5 9.2 fusion.3
  307.7 8.5 fusion.31
  326.4 38.9 %collective-permute-done.1 = bf16[1458,576]{0,1:T(8,128)(2,1)} collective-permute-done((bf16[1458,576]{0,1:T(8,128)(2,1)S(1)}, bf16[1458,576]{0,1:T(8,128)(2,1)}, u32[]{:S(2)}, u32[]{:S(2)}) %collective-permute-start.1) | collective-permute-done | bytes 1679648 | tf_op jit(solution)/shard_map/ppermute | solution.py:89
  378.2 13.9 fusion.52
  392.1 33.4 %all-reduce.26.cloned.1.call-done = bf16[2916,288]{0,1:T(8,128)(2,1)} async-done(((bf16[2916,288]{0,1:T(8,128)(2,1)}), bf16[2916,288]{0,1:T(8,128)(2,1)}) %all-reduce.26.cloned.1.call-update) | async-done | bytes 1679632
  427.5 10.7 all-reduce.17
  441.6 218.2 %fusion.2 = f32[736,2152]{1,0:T(8,128)} fusion(f32[2916,2152]{1,0:T(8,128)} %fusion.52), kind=kCustom, calls=%all-reduce-scatter.2 | all-reduce-scatter fusion | flops 6335489 | bytes 31436928
  672.1 13.1 fusion.51
  685.3 219.9 %fusion.1 = f32[736,2152]{1,0:T(8,128)} fusion(f32[2916,2152]{1,0:T(8,128)} %fusion.51), kind=kCustom, calls=%all-reduce-scatter.1 | all-reduce-scatter fusion | flops 6335489 | bytes 31436928
  907.5 17.6 concatenate.36
  925.1 17.5 concatenate.35
  942.6 12.3 convert_reduce_fusion
  956.5 5.6 collective-permute-done.2
  962.1 9.0 maximum_select_fusion.1
  971.4 128.7 %all-gather.19.cloned.1.call-done = bf16[4,729,2152]{2,1,0:T(8,128)(2,1)} async-done(((bf16[1,729,2152]{2,1,0:T(8,128)(2,1)}), bf16[4,729,2152]{2,1,0:T(8,128)(2,1)}) %all-gather.19.cloned.1.call-update) | async-done | bytes 12550480 | tf_op jit(solution)/shard_map/all_gather | solution.py:71
  1100.1 16.9 reshape.99
  1117.0 10.6 fusion.53
  1127.9 44.9 %collective-permute-done.3 = bf16[1458,2152]{1,0:T(8,128)(2,1)} collective-permute-done((bf16[1458,2152]{1,0:T(8,128)(2,1)}, bf16[1458,2152]{1,0:T(8,128)(2,1)}, u32[]{:S(2)}, u32[]{:S(2)}) %collective-permute-start.3) | collective-permute-done | bytes 6275264 | tf_op jit(solution)/shard_map/ppermute | solution.py:89
  1172.9 17.1 convolution_convert_fusion.2
  1190.0 30.3 %all-reduce.30.cloned.1.call-done = f32[2916,288]{0,1:T(8,128)} async-done(((f32[2916,288]{0,1:T(8,128)}), f32[2916,288]{0,1:T(8,128)}) %all-reduce.30.cloned.1.call-update) | async-done | bytes 3359248
  1223.7 11.1 all-reduce.16
  1234.8 42.1 %all-reduce.28.cloned.1.call-done = bf16[2916,288]{0,1:T(8,128)(2,1)} async-done(((bf16[2916,288]{0,1:T(8,128)(2,1)}), bf16[2916,288]{0,1:T(8,128)(2,1)}) %all-reduce.28.cloned.1.call-update) | async-done | bytes 1679632
  1285.4 28.9 %all-gather.21.cloned.1.call-done = bf16[2,1458,288]{1,2,0:T(8,128)(2,1)} async-done(((bf16[1,1458,288]{1,2,0:T(8,128)(2,1)}), bf16[2,1458,288]{1,2,0:T(8,128)(2,1)}) %all-gather.21.cloned.1.call-update) | async-done | bytes 1679632 | tf_op jit(solution)/shard_map/all_gather | solution.py:43
  1324.2 6.2 fusion.54
  1330.4 120.4 %all-reduce.35 = bf16[2916,576]{0,1:T(8,128)(2,1)} all-reduce(f32[2916,576]{0,1:T(8,128)} %fusion.54), channel_id=8, replica_groups=mesh['dp'=4,'row'=4,'col'=2] {'row'}, use_global_device_ids=true, to_apply=%region_20.21.clone | all-reduce | flops 1679616 | bytes 10077696
  1452.5 12.2 multiply_reduce_fusion
  1464.7 12.8 multiply_convert_fusion
  1481.9 7.9 fusion.32
  1497.6 16.5 convolution_convert_fusion
  1514.2 10.5 convolution_convert_fusion.1
  1524.9 6.7 convolution_convert_fusion.5
  1531.8 35.6 %all-gather.23.cloned.1.call-done = bf16[4,729,1728]{2,1,0:T(8,128)(2,1)} async-done(((bf16[1,729,1728]{2,1,0:T(8,128)(2,1)}), bf16[4,729,1728]{2,1,0:T(8,128)(2,1)}) %all-gather.23.cloned.1.call-update) | async-done | bytes 10077712 | tf_op jit(solution)/shard_map/all_gather | solution.py:71
  1567.4 14.8 reshape.103
  1582.2 8.9 convolution_convert_fusion.4
  1598.2 9.6 fusion.55
  1611.9 19.5 %reduce-scatter.21.cloned.1.call-done = bf16[72,2152]{1,0:T(8,128)(2,1)} async-done(((bf16[288,2152]{1,0:T(8,128)(2,1)}), bf16[72,2152]{1,0:T(8,128)(2,1)}) %reduce-scatter.21.cloned.1.call-update) | async-done | bytes 309904
  1635.2 19.0 %reduce-scatter.19.cloned.1.call-done = bf16[144,288]{1,0:T(8,128)(2,1)} async-done(((bf16[576,288]{1,0:T(8,128)(2,1)}), bf16[144,288]{1,0:T(8,128)(2,1)}) %reduce-scatter.19.cloned.1.call-update) | async-done | bytes 82960 | tf_op jit(solution)/shard_map/reduce_scatter | solution.py:243
  1655.8 64.9 %all-reduce.34.cloned.1.call-done = bf16[288,3,576]{2,1,0:T(4,128)(2,1)} async-done(((bf16[288,3,576]{2,1,0:T(4,128)(2,1)}), bf16[288,3,576]{2,1,0:T(4,128)(2,1)}) %all-reduce.34.cloned.1.call-update) | async-done | bytes 995344
  1722.6 90.7 %all-reduce.32.cloned.1.call-done = f32[2916,288]{0,1:T(8,128)} async-done(((f32[2916,288]{0,1:T(8,128)}), f32[2916,288]{0,1:T(8,128)}) %all-reduce.32.cloned.1.call-update) | async-done | bytes 3359248
  1816.4 40.5 %all-reduce.14 = (f32[6,1152]{1,0:T(8,128)S(1)}, f32[2,1152]{1,0:T(2,128)S(1)}, f32[4304]{0:T(1024)S(1)}) all-reduce(f32[6,1152]{1,0:T(8,128)S(1)} %dynamic_update_slice.18, f32[2,1152]{1,0:T(2,128)S(1)} %dynamic_update_slice.19, f32[4304]{0:T(1024)S(1)} %dynamic_update_slice.20), channel_id=1, replica_groups=mesh['dp'=4,'row'=4,'col'=2] {'dp','row','col'}, use_global_device_ids=true, to_apply=%region_33.34 | all-reduce | flops 13520 | bytes 108160 | tf_op jit(solution)/shard_map/psum | solution.py:234
  1858.3 10.9 all-reduce.15
  (174 shorter events, 135.4 us)
Async XLA Ops:
  7.2 665.0 %copy-start = (bf16[288,2152]{1,0:T(8,128)(2,1)S(1)}, bf16[288,2152]{1,0:T(8,128)(2,1)}, u32[]{:S(2)}) copy-start(bf16[288,2152]{1,0:T(8,128)(2,1)} %param.19) | copy-start | bytes 3718660
  7.2 18.9 %copy-start.11 = (bf16[288,3,576]{2,0,1:T(8,128)(2,1)S(1)}, bf16[288,3,576]{2,0,1:T(8,128)(2,1)}, u32[]{:S(2)}) copy-start(bf16[288,3,576]{2,0,1:T(8,128)(2,1)} %param.15) | copy-start | bytes 2985988
  7.2 20.5 %copy-start.21 = (bf16[2,576]{1,0:T(2,128)(2,1)S(1)}, bf16[2,576]{1,0:T(2,128)(2,1)}, u32[]{:S(2)}) copy-start(bf16[2,576]{1,0:T(2,128)(2,1)} %param.16) | copy-start | bytes 6916
  7.2 48.7 %all-gather.13.cloned.1.call-start = ((), (), s32[]{:S(2)}) async-start(), calls=%async_computation.4 | async-start | bytes 2654208 | tf_op jit(solution)/shard_map/all_gather | solution.py:43
  22.9 0.6 copy-start.14
  22.9 0.6 copy-start.16
  26.0 346.4 %all-gather.17.cloned.1.call-start = ((), (), s32[]{:S(2)}) async-start(), calls=%async_computation.6 | async-start | bytes 2654208 | tf_op jit(solution)/shard_map/all_gather | solution.py:43
  64.9 12.0 copy-start.6
  76.9 184.3 %copy-start.23 = (u32[32]{0:T(128)S(1)}, u32[32]{0:T(128)}, u32[]{:S(2)}) copy-start(u32[32]{0:T(128)} %constant.92) | copy-start | bytes 388
  259.3 3.2 collective-permute-start.4
  290.9 7.5 copy-start.3
  316.2 2.0 copy-start.12
  316.2 49.1 %copy-start.13 = (bf16[576,288]{0,1:T(8,128)(2,1)S(1)}, bf16[576,288]{0,1:T(8,128)(2,1)}, u32[]{:S(2)}) copy-start(bf16[576,288]{0,1:T(8,128)(2,1)} %param.17) | copy-start | bytes 995332
  316.2 4.1 collective-permute-start
  323.5 47.4 %copy-start.9 = (bf16[1458,576]{0,1:T(8,128)(2,1)}, bf16[1458,576]{0,1:T(8,128)(2,1)S(1)}, u32[]{:S(2)}) copy-start(bf16[1458,576]{0,1:T(8,128)(2,1)S(1)} %maximum_select_fusion.5) | copy-start | bytes 5038852
  323.5 41.8 %collective-permute-start.1 = (bf16[1458,576]{0,1:T(8,128)(2,1)S(1)}, bf16[1458,576]{0,1:T(8,128)(2,1)}, u32[]{:S(2)}, u32[]{:S(2)}) collective-permute-start(bf16[1458,576]{0,1:T(8,128)(2,1)S(1)} %maximum_select_fusion.5), channel_id=1, source_target_pairs={{0,4},{2,6},{4,0},{6,2},{1,5},{3,7},{5,1},{7,3},{8,12},{10,14},{12... | collective-permute-start | bytes 5038856 | tf_op jit(solution)/shard_map/ppermute | solution.py:89
  326.3 99.2 %all-reduce.26.cloned.1.call-start = ((), (), s32[]{:S(2)}) async-start(), calls=%async_computation.10 | async-start | bytes 3391488
  326.4 44.7 %copy-start.27 = (u32[32]{0:T(128)S(1)}, u32[32]{0:T(128)}, u32[]{:S(2)}) copy-start(u32[32]{0:T(128)} %constant.96) | copy-start | bytes 388
  326.4 45.3 %copy-start.24 = (bf16[288]{0:T(512)(128)(2,1)S(1)}, bf16[288]{0:T(512)(128)(2,1)}, u32[]{:S(2)}) copy-start(bf16[288]{0:T(512)(128)(2,1)} %param.18) | copy-start | bytes 1732
  370.9 291.4 %all-gather.15.cloned.1.call-start = ((), (), s32[]{:S(2)}) async-start(), calls=%async_computation.5 | async-start | bytes 2654208 | tf_op jit(solution)/shard_map/all_gather | solution.py:43
  378.2 47.4 %copy-start.2 = (bf16[1458,288]{0,1:T(8,128)(2,1)S(1)}, bf16[1458,288]{0,1:T(8,128)(2,1)}, u32[]{:S(2)}) copy-start(bf16[1458,288]{0,1:T(8,128)(2,1)} %param.12) | copy-start | bytes 2519428
  441.6 658.6 %all-gather.19.cloned.1.call-start = ((), (), s32[]{:S(2)}) async-start(), calls=%async_computation.7 | async-start | bytes 16015360 | tf_op jit(solution)/shard_map/all_gather | solution.py:71
  660.7 246.7 %collective-permute-start.6 = (f32[21,2152]{1,0:T(8,128)S(1)}, f32[21,2152]{1,0:T(8,128)S(1)}, u32[]{:S(2)}, u32[]{:S(2)}) collective-permute-start(f32[21,2152]{1,0:T(8,128)S(1)} %slice.78), channel_id=1, source_target_pairs={{0,2},{2,4},{4,6},{1,3},{3,5},{5,7},{8,10},{10,12},{12,14},{9,11},... | collective-permute-start | bytes 542312
  685.3 222.2 %copy-start.22 = (bf16[2152]{0:T(1024)(128)(2,1)S(1)}, bf16[2152]{0:T(1024)(128)(2,1)}, u32[]{:S(2)}) copy-start(bf16[2152]{0:T(1024)(128)(2,1)} %param.20) | copy-start | bytes 12916
  906.1 18.9 %collective-permute-start.5 = (f32[21,2152]{1,0:T(8,128)S(1)}, f32[21,2152]{1,0:T(8,128)S(1)}, u32[]{:S(2)}, u32[]{:S(2)}) collective-permute-start(f32[21,2152]{1,0:T(8,128)S(1)} %slice.77), channel_id=1, source_target_pairs={{0,2},{2,4},{4,6},{1,3},{3,5},{5,7},{8,10},{10,12},{12,14},{9,11},... | collective-permute-start | bytes 542312
  954.9 265.5 %all-reduce.30.cloned.1.call-start = ((), (), s32[]{:S(2)}) async-start(), calls=%async_computation.12 | async-start | bytes 6782976
  955.4 6.7 collective-permute-start.2
  971.1 201.7 %collective-permute-start.3 = (bf16[1458,2152]{1,0:T(8,128)(2,1)}, bf16[1458,2152]{1,0:T(8,128)(2,1)}, u32[]{:S(2)}, u32[]{:S(2)}) collective-permute-start(bf16[1458,2152]{1,0:T(8,128)(2,1)} %maximum_select_fusion.1), channel_id=1, source_target_pairs={{0,4},{2,6},{4,0},{6,2},{1,5},{3,7},{5,1},{7,3},{8,12},{10,14},{12... | collective-permute-start | bytes 18825704 | tf_op jit(solution)/shard_map/ppermute | solution.py:89
  1127.7 45.2 %copy-start.10 = (bf16[2152,288]{0,1:T(8,128)(2,1)S(1)}, bf16[2152,288]{0,1:T(8,128)(2,1)}, u32[]{:S(2)}) copy-start(bf16[2152,288]{0,1:T(8,128)(2,1)} %param.21) | copy-start | bytes 3718660
  1127.7 62.3 %copy-start.25 = (bf16[288]{0:T(512)(128)(2,1)S(1)}, bf16[288]{0:T(512)(128)(2,1)}, u32[]{:S(2)}) copy-start(bf16[288]{0:T(512)(128)(2,1)} %param.22) | copy-start | bytes 1732
  1127.7 149.2 %all-reduce.28.cloned.1.call-start = ((), (), s32[]{:S(2)}) async-start(), calls=%async_computation.11 | async-start | bytes 3391488
  1189.9 87.0 %copy-start.8 = (bf16[1458,288]{0,1:T(8,128)(2,1)S(1)}, bf16[1458,288]{0,1:T(8,128)(2,1)}, u32[]{:S(2)}) copy-start(bf16[1458,288]{0,1:T(8,128)(2,1)} %param.23) | copy-start | bytes 2519428
  1190.0 124.3 %all-gather.21.cloned.1.call-start = ((), (), s32[]{:S(2)}) async-start(), calls=%async_computation.8 | async-start | bytes 2654208 | tf_op jit(solution)/shard_map/all_gather | solution.py:43
  1282.3 1.3 copy-start.5
  1284.7 282.7 %all-gather.23.cloned.1.call-start = ((), (), s32[]{:S(2)}) async-start(), calls=%async_computation.9 | async-start | bytes 13189120 | tf_op jit(solution)/shard_map/all_gather | solution.py:71
  1464.7 12.8 copy-start.4
  1489.8 0.9 copy-start.7
  1497.2 112.9 %reduce-scatter.23.cloned.1.call-start = ((), (), s32[]{:S(2)}) async-start(), calls=%async_computation.16 | async-start | bytes 1566720
  1514.2 117.2 %reduce-scatter.21.cloned.1.call-start = ((), (), s32[]{:S(2)}) async-start(), calls=%async_computation.15 | async-start | bytes 1566720
  1524.8 129.4 %reduce-scatter.19.cloned.1.call-start = ((), (), s32[]{:S(2)}) async-start(), calls=%async_computation.3 | async-start | bytes 552960 | tf_op jit(solution)/shard_map/reduce_scatter | solution.py:243
  1531.5 189.1 %all-reduce.34.cloned.1.call-start = ((), (), s32[]{:S(2)}) async-start(), calls=%async_computation.14 | async-start | bytes 2949120
  1597.9 215.4 %all-reduce.32.cloned.1.call-start = ((), (), s32[]{:S(2)}) async-start(), calls=%async_computation.13 | async-start | bytes 6782976
  1607.8 0.7 copy-start.26
  1607.8 1.9 copy-start.18
  1611.9 201.4 %copy-start.15 = (f32[1458]{0:T(1024)S(1)}, f32[1458]{0:T(1024)}, u32[]{:S(2)}) copy-start(f32[1458]{0:T(1024)} %copy-done.14) | copy-start | bytes 17500
  1611.9 201.5 %copy-start.17 = (f32[1458]{0:T(1024)S(1)}, f32[1458]{0:T(1024)}, u32[]{:S(2)}) copy-start(f32[1458]{0:T(1024)} %copy-done.16) | copy-start | bytes 17500
  1611.9 201.5 %copy-start.20 = (f32[288]{0:T(512)S(1)}, f32[288]{0:T(512)}, u32[]{:S(2)}) copy-start(f32[288]{0:T(512)} %copy-done.19) | copy-start | bytes 3460
  1813.3 61.0 %copy-start.1 = (bf16[288,2152]{1,0:T(8,128)(2,1)S(1)}, bf16[288,2152]{1,0:T(8,128)(2,1)}, u32[]{:S(2)}) copy-start(bf16[288,2152]{1,0:T(8,128)(2,1)} %param.19) | copy-start | bytes 3718660
  (1 other events, 0.6 us)
Sparse Core Ops, SparseCore 0:
  26.1 29.7 all-gather.12
  326.5 28.4 all-gather.16
  371.0 54.5 all-reduce.25
  441.7 29.0 all-gather.14
  955.0 145.0 all-gather.18
  1127.8 92.5 all-reduce.29
  1222.7 54.1 all-reduce.27
  1284.8 29.4 all-gather.20
  1497.3 70.0 all-gather.22
  1569.5 30.2 reduce-scatter.22
  1602.1 29.1 reduce-scatter.20
  1634.1 20.1 reduce-scatter.18
  1656.6 64.0 all-reduce.33
  1722.9 90.4 all-reduce.31
